TPU v7x, 256 devices: a whole 4x4x8 slice. The times are simulated.
256 devices in a mesh: ctx: 32 (over z, x_hi, core), tp: 8 (over y, x_lo).
Axes of the slice: x: 4 (x_hi: 2, x_lo: 2; x = x_hi * 2 + x_lo), y: 4, z: 8, core: 2. Of those that a mesh axis runs over, the one named last changes fastest.
Arguments:
- compressed: bfloat16 [4096, 1536], P('ctx', 'tp'), may hold values from -6 to 6
- latent: bfloat16 [4096, 576], P('ctx'), may hold values from -276 to 276
- w_uq: bfloat16 [1536, 12288], P(None, 'tp'), may hold values from -0.15625 to 0.15625
- w_uk: bfloat16 [512, 8192], P('ctx', 'tp'), may hold values from -0.5 to 0.5
- w_uv: bfloat16 [512, 8192], P('ctx', 'tp'), may hold values from -0.8984375 to 0.8984375
- span_ids: int32 [64], replicated, may hold values from 0 to 63, as said below
Outputs:
- attended: bfloat16 [4096, 8192], P('ctx', 'tp')
Inputs may be any that keep to these rules, and one draw needn't show every extreme that they name: `span_ids`: entries 2 d and 2 d + 1 hold spans c and 63 - c for some c < 32, in that order; every span appears once.
All inputs are finite; a program needn't handle non-finite values.
Results may differ from a plain program's by a relative error of at most 0.0085.
The roundings to bfloat16 on the way count: a program that leaves them out, or rounds other values in their place, can miss the bound.
Values may be sent and summed in bfloat16 or wider, within the bound.
No kernel may reach another device: no remote copies, remote signals or barrier semaphores. Data moves between devices by JAX's collectives and lax.ppermute only.
A program may use at most 64 MiB of HBM per device.

v0:
```python
import jax
import jax.numpy as jnp
from jax import lax
from jax.sharding import PartitionSpec as P

NOPE = 128
ROPE = 64
VDIM = 128
KV = 512


def per_device(compressed, latent, w_uq, w_uk, w_uv, span_ids):
    row_count = compressed.shape[0]
    span_len = row_count // 2
    heads_dev = w_uk.shape[1] // NOPE
    span_count = span_ids.shape[0]
    total_slots = span_count * span_len
    softmax_scale = (NOPE + ROPE) ** (-0.5)
    query_proj = jnp.dot(
        lax.all_gather(compressed, "tp", axis=1, tiled=True),
        w_uq,
        preferred_element_type=jnp.float32,
    )
    query_proj = query_proj.astype(jnp.bfloat16).reshape(row_count, heads_dev, NOPE + ROPE)
    q_nope = query_proj[:, :, :NOPE]
    q_rope = query_proj[:, :, NOPE:]
    shard_rows = lax.all_gather(w_uk, "ctx", axis=0, tiled=True)
    key_block = shard_rows.reshape(shard_rows.shape[0], heads_dev, NOPE)
    q_latent = jnp.einsum(
        "rhk,chk->rhc", q_nope, key_block, preferred_element_type=jnp.float32
    ).astype(jnp.bfloat16)
    q_full = jnp.concatenate([q_latent, q_rope], axis=2)
    positions = jnp.repeat(
        span_ids, span_len, total_repeat_length=total_slots
    ) * span_len + jnp.tile(jnp.arange(span_len, dtype=jnp.int32), span_count)
    q_positions = lax.dynamic_slice_in_dim(positions, lax.axis_index("ctx") * row_count, row_count)
    queries = [
        q_full[slot_j * span_len : (slot_j + 1) * span_len].reshape(span_len * heads_dev, KV + ROPE)
        for slot_j in range(2)
    ]
    query_pos = [q_positions[slot_j * span_len : (slot_j + 1) * span_len] for slot_j in range(2)]

    def update(state, q_matrix, q_pos, key_rows, key_pos):
        highest, totals, running = state
        scores = (
            lax.dot_general(
                q_matrix, key_rows, (((1,), (1,)), ((), ())), preferred_element_type=jnp.float32
            )
            * softmax_scale
        )
        visible = key_pos[None, :] <= q_pos[:, None]
        visible = jnp.broadcast_to(
            visible[:, None, :], (q_pos.shape[0], heads_dev, key_pos.shape[0])
        ).reshape(q_matrix.shape[0], key_pos.shape[0])
        scores = jnp.where(visible, scores, -1e30)
        new_high = jnp.maximum(highest, jnp.max(scores, axis=1))
        weights = jnp.where(visible, jnp.exp(scores - new_high[:, None]), 0.0)
        totals = jnp.sum(weights, axis=1)
        running = jnp.dot(
            weights.astype(jnp.bfloat16), key_rows[:, :KV], preferred_element_type=jnp.float32
        )
        return (new_high, totals, running)

    def visit_span(state, slot_j, key_rows, key_pos):
        return lax.cond(
            jnp.min(key_pos) <= jnp.max(query_pos[slot_j]),
            lambda inner: update(inner, queries[slot_j], query_pos[slot_j], key_rows, key_pos),
            lambda inner: inner,
            state,
        )

    score_rows = span_len * heads_dev
    initial = tuple(
        (
            (
                jnp.full((score_rows,), -1e30, jnp.float32),
                jnp.zeros((score_rows,), jnp.float32),
                jnp.zeros((score_rows, KV), jnp.float32),
            )
            for slot_j in range(2)
        )
    )

    def fold_keys(states, shard_rows):
        key_pos = lax.slice_in_dim(positions, 0, shard_rows.shape[0], axis=0)
        return tuple(
            (visit_span(states[slot_j], slot_j, shard_rows, key_pos) for slot_j in range(2))
        )

    states = fold_keys(initial, lax.all_gather(latent, "ctx", axis=0, tiled=True))
    mixed = jnp.concatenate(
        [
            (states[slot_j][2] / states[slot_j][1][:, None])
            .astype(jnp.bfloat16)
            .reshape(span_len, heads_dev, KV)
            for slot_j in range(2)
        ],
        axis=0,
    )
    shard_rows = lax.all_gather(w_uv, "ctx", axis=0, tiled=True)
    value_block = shard_rows.reshape(shard_rows.shape[0], heads_dev, VDIM)
    result = jnp.einsum("rhc,chv->rhv", mixed, value_block, preferred_element_type=jnp.float32)
    return result.reshape(row_count, heads_dev * VDIM).astype(jnp.bfloat16)


def solution(mesh):
    placed = (P("ctx", "tp"), P("ctx", None), P(None, "tp"), P("ctx", "tp"), P("ctx", "tp"), P())
    return jax.shard_map(
        per_device, mesh=mesh, in_specs=placed, out_specs=P("ctx", "tp"), check_vma=False
    )
```

profile of v0, /device:TPU:1, one launch (start us, length us, event | category | flops | bytes accessed | tf_op | source)
XLA Modules:
  0.0 294.5 jit_solution(12755800408900300186)
XLA Ops:
  6.5 0.7 all-gather.4.cloned.1.call-update
  7.3 0.7 all-gather.8.cloned.1.call-update
  8.1 1.7 copy.31
  9.8 0.1 tile.14
  9.9 25.2 %all_gather.12 = bf16[128,1536]{0,1:T(8,128)(2,1)S(1)} all-gather(bf16[128,192]{0,1:T(8,128)(2,1)} %param.12), channel_id=1, replica_groups=mesh['ctx'=32,'tp'=8] {'tp'}, dimensions={1}, use_global_device_ids=true | all-gather | bytes 442368 | tf_op jit(solution)/shard_map/all_gather | solution.py:20
  35.1 3.2 %convolution_convert_fusion = bf16[128,1536]{1,0:T(8,128)(2,1)S(1)} fusion(bf16[128,1536]{0,1:T(8,128)(2,1)S(1)} %all_gather.12, bf16[1536,1536]{1,0:T(8,128)(2,1)} %param.14), kind=kOutput, calls=%fused_computation.38 | convolution fusion | flops 604176384 | bytes 5505024 | tf_op jit(solution)/shard_map/dot_general | solution.py:19
  38.3 0.2 copy.26
  38.5 0.2 copy.40
  38.7 0.1 broadcast.180
  38.8 0.1 reshape.182
  38.9 0.8 add_add_fusion.1
  39.7 0.1 add.86
  39.8 0.1 sub.31
  39.9 1.6 fusion.41
  41.5 2.1 fusion.38
  43.5 2.1 fusion.39
  45.6 2.1 fusion.40
  47.7 0.8 add_add_fusion.3
  48.5 4.5 %compare_select_fusion.1 = (s32[4096,1]{0,1:T(1,128)S(1)}, s32[4096,1]{0,1:T(1,128)S(1)}) fusion(s32[]{:T(128)} %bitcast.63, s32[]{:T(128)} %bitcast.64, s32[]{:T(128)} %bitcast.65, s32[]{:T(128)} %bitcast.66, s32[]{:T(128)} %bitcast.67, s32[]{:T(128)} %bitcast.69, s32[]{:T(128)} %bitcast.68, s32[4096,1]{0,1:T(1,128)S(1)} %bitcast.133, ...), kind=kLoop, calls=%fused_computation.109 | loop fusion | flops 57344 | bytes 65564 | tf_op jit(solution)/shard_map/jit(_take)/gather | solution.py:33
  53.0 2.9 compare_reduce_fusion.56
  55.9 35.8 %multiply_add_fusion = (s32[4096]{0:T(1024)S(1)}, s32[4096]{0:T(1024)S(1)}) fusion(s32[4096]{0:T(1024)S(1)} %tile.14, s32[32,128]{1,0:T(8,128)S(1)} %copy-done.1, s32[32]{0:T(128)S(1)} %iota_multiply_fusion, pred[4096]{0:T(1024)(128)(4,1)S(1)} %get-tuple-element.133, pred[4096]{0:T(1024)(128)(4,1)S(1)} %get-tuple-element.132, ...), kind=kLoop, calls=%fused_computation.122 | loop fusion | flops 278528 | bytes 315748 | tf_op jit(solution)/shard_map/add | solution.py:33
  91.7 0.1 dynamic_slice.3
  91.8 0.6 add_reduce_fusion
  92.4 0.7 slice_reduce_fusion.1
  95.7 1.5 copy.28
  97.2 72.0 %all-gather.8.cloned.1.call-done = bf16[512,1024]{1,0:T(8,128)(2,1)} async-done(((bf16[16,1024]{1,0:T(8,128)(2,1)}), bf16[512,1024]{1,0:T(8,128)(2,1)}) %all-gather.8.cloned.1.call-update) | async-done | bytes 1048592 | tf_op jit(solution)/shard_map/all_gather | solution.py:100
  169.2 2.3 copy.36
  171.5 0.5 fusion.30
  172.0 0.1 pad_maximum_fusion
  172.1 87.4 %all-gather.6.cloned.1.call-done = bf16[4096,576]{1,0:T(8,128)(2,1)} async-done(((bf16[128,576]{1,0:T(8,128)(2,1)}), bf16[4096,576]{1,0:T(8,128)(2,1)}) %all-gather.6.cloned.1.call-update) | async-done | bytes 4718608 | tf_op jit(solution)/shard_map/all_gather | solution.py:90
  259.5 13.2 %conditional.2 = (f32[512]{0:T(512)S(1)}, f32[512,512]{1,0:T(8,128)S(1)}) conditional(s32[]{:T(128)} %convert_element_type.36, () %tuple.25, (s32[4096]{0:T(1024)S(1)}, s32[64]{0:T(128)S(1)}, bf16[128,8,576]{2,0,1:T(8,128)(2,1)S(1)}, bf16[4096,576]{1,0:T(8,128)(2,1)}) %tuple.26), branch_computations={%region_2.3_spmd, %region_3.6_spmd} | conditional | flops 4590927360 | bytes 54948160 | solution.py:65
  259.5 0.2 broadcast_compare_fusion
  259.7 0.7 copy.32
  260.5 6.5 %fusion = (f32[512]{0:T(512)S(1)}, f32[512,4096]{1,0:T(8,128)S(1)}) fusion(pred[64,4096]{1,0:T(8,128)(4,1)S(1)} %broadcast_compare_fusion, bf16[4096,576]{1,0:T(8,128)(2,1)} %get-tuple-element.40, bf16[128,8,576]{2,1,0:T(8,128)(2,1)S(1)} %copy.32), kind=kOutput, calls=%fused_computation.2 | convolution fusion | flops 2422210048 | bytes 14026752 | tf_op jit(solution)/shard_map/cond/branch_1_fun/dot_general | solution.py:46
  267.1 2.6 fusion.3
  269.6 3.1 %fusion.2 = f32[512]{0:T(512)S(1)} fusion(f32[512,4096]{1,0:T(8,128)S(1)} %get-tuple-element.141, f32[512]{0:T(512)S(1)} %broadcast_maximum_fusion, pred[64,4096]{1,0:T(8,128)(4,1)S(1)} %broadcast_compare_fusion), kind=kLoop, calls=%fused_computation.4 | loop fusion | flops 10485248 | bytes 8654848 | tf_op jit(solution)/shard_map/cond/branch_1_fun/reduce_sum | solution.py:58
  272.7 0.1 fusion.34
  272.8 0.2 copy.34
  273.0 13.3 %conditional.3 = (f32[512]{0:T(512)S(1)}, f32[512,512]{1,0:T(8,128)S(1)}) conditional(s32[]{:T(128)} %convert_element_type.41, () %tuple.27, (s32[4096]{0:T(1024)S(1)}, s32[64]{0:T(128)S(1)}, bf16[128,8,576]{2,0,1:T(8,128)(2,1)S(1)}, bf16[4096,576]{1,0:T(8,128)(2,1)}) %tuple.28), branch_computations={%region_7.8_spmd, %region_8.11_spmd} | conditional | flops 4590927360 | bytes 54948160 | solution.py:65
  273.3 0.2 broadcast_compare_fusion.1
  273.5 0.7 copy.33
  274.2 6.5 %fusion.15 = (f32[512]{0:T(512)S(1)}, f32[512,4096]{1,0:T(8,128)S(1)}) fusion(pred[64,4096]{1,0:T(8,128)(4,1)S(1)} %broadcast_compare_fusion.1, bf16[4096,576]{1,0:T(8,128)(2,1)} %get-tuple-element.44, bf16[128,8,576]{2,1,0:T(8,128)(2,1)S(1)} %copy.33), kind=kOutput, calls=%fused_computation.21 | convolution fusion | flops 2422210048 | bytes 14026752 | tf_op jit(solution)/shard_map/cond/branch_1_fun/dot_general | solution.py:46
  280.8 2.5 fusion.18
  283.3 2.9 %fusion.17 = f32[512]{0:T(512)S(1)} fusion(f32[512,4096]{1,0:T(8,128)S(1)} %get-tuple-element.143, f32[512]{0:T(512)S(1)} %broadcast_maximum_fusion.1, pred[64,4096]{1,0:T(8,128)(4,1)S(1)} %broadcast_compare_fusion.1), kind=kLoop, calls=%fused_computation.23 | loop fusion | flops 10485248 | bytes 8654848 | tf_op jit(solution)/shard_map/cond/branch_1_fun/reduce_sum | solution.py:58
  286.3 0.1 fusion.35
  286.4 0.2 copy.35
  286.6 0.5 convolution_convert_fusion.2
  287.1 0.9 copy.37
  (24 shorter events, 0.2 us)
Async XLA Ops:
  6.5 49.4 %copy-start.1 = (s32[32,128]{1,0:T(8,128)S(1)}, s32[32,128]{1,0:T(8,128)}, u32[]{:S(2)}) copy-start(s32[32,128]{1,0:T(8,128)} %constant.125.clone.1) | copy-start | bytes 49156
  6.5 89.1 %all-gather.4.cloned.1.call-start = ((), (), s32[]{:S(2)}) async-start(), calls=%async_computation | async-start | bytes 1081344 | tf_op jit(solution)/shard_map/all_gather | solution.py:27
  7.3 161.9 %all-gather.8.cloned.1.call-start = ((), (), s32[]{:S(2)}) async-start(), calls=%async_computation.2 | async-start | bytes 1081344 | tf_op jit(solution)/shard_map/all_gather | solution.py:100
  8.0 251.5 %all-gather.6.cloned.1.call-start = ((), (), s32[]{:S(2)}) async-start(), calls=%async_computation.1 | async-start | bytes 5406720 | tf_op jit(solution)/shard_map/all_gather | solution.py:90
  259.7 7.3 %slice-start = ((s8[5242880]{0:T(1024)(128)(4,1)}), s8[4194304]{0:T(1024)(128)(4,1)S(1)}, s32[]{:S(2)}) async-start(s8[5242880]{0:T(1024)(128)(4,1)} %bitcast.135), calls=%async_computation.3 | async-start | bytes 8388608 | tf_op jit(solution)/shard_map/cond
  260.5 6.6 %slice-start.1 = ((s8[5242880]{0:T(1024)(128)(4,1)}), s8[1048576]{0:T(1024)(128)(4,1)S(1)}, s32[]{:S(2)}) async-start(s8[5242880]{0:T(1024)(128)(4,1)} %bitcast.135), calls=%async_computation.4 | async-start | bytes 2097152 | tf_op jit(solution)/shard_map/cond
  273.0 13.6 %copy-start = (bf16[512,1024]{0,1:T(8,128)(2,1)S(1)}, bf16[512,1024]{0,1:T(8,128)(2,1)}, u32[]{:S(2)}) copy-start(bf16[512,1024]{0,1:T(8,128)(2,1)} %copy.36) | copy-start | bytes 3145732
  273.5 7.3 %slice-start.2 = ((s8[5242880]{0:T(1024)(128)(4,1)}), s8[4194304]{0:T(1024)(128)(4,1)S(1)}, s32[]{:S(2)}) async-start(s8[5242880]{0:T(1024)(128)(4,1)} %bitcast.137), calls=%async_computation.5 | async-start | bytes 8388608 | tf_op jit(solution)/shard_map/cond
  274.2 6.6 %slice-start.3 = ((s8[5242880]{0:T(1024)(128)(4,1)}), s8[1048576]{0:T(1024)(128)(4,1)S(1)}, s32[]{:S(2)}) async-start(s8[5242880]{0:T(1024)(128)(4,1)} %bitcast.137), calls=%async_computation.6 | async-start | bytes 2097152 | tf_op jit(solution)/shard_map/cond
Sparse Core Ops, SparseCore 0:
  10.1 81.7 all-gather.3
  94.7 74.4 all-gather.7
  172.0 87.5 all-gather.5
where the time goes:
time: 295 us; the launch traced here: 294 us
  waiting for transfers between devices  161 us (55%)
  other arithmetic  53 us (18%)
  blocking collectives  25.2 us (9%)
  matrix products  22.2 us (8%)
  local copies, waits for them, and re-layouts  16.9 us (6%)
  between operations  15.7 us (5%)
    all_gather x1, waiting for transfers between devices, per_device(): lax.all_gather(latent, 'ctx', axis=0, tiled=True)  87.4 us
    all_gather x1, waiting for transfers between devices, per_device(): shard_rows = lax.all_gather(w_uv, 'ctx', axis=0, tiled=True)  72 us
    add x1, other arithmetic, per_device(): jnp.repeat(span_ids, span_len, total_repeat_length=total_slots) * span_len  35.8 us
    all_gather x1, blocking collectives, per_device(): lax.all_gather(compressed, 'tp', axis=1, tiled=True)  25.2 us
    dot_general x2, matrix products, update(): lax.dot_general(q_matrix, key_rows, (((1,), (1,)), ((), ())), preferred_e...  13.1 us
    gather x4, local copies, waits for them, and re-layouts, per_device(): jnp.repeat(span_ids, span_len, total_repeat_length=total_slots) * span_len  7.81 us
    gather x2, other arithmetic, per_device(): jnp.repeat(span_ids, span_len, total_repeat_length=total_slots) * span_len  7.4 us
    reduce_sum x2, other arithmetic, update(): totals = jnp.sum(weights, axis=1)  6.01 us
  transfers between devices with their start and end apart: 3, of which 2 were waited for; matrix products, arithmetic and copies ran while one was open for 22% of the time, Pallas kernels for 0%

commit v1 on v0

--- a/solution.py
+++ b/solution.py
@@ -17,7 +17,9 @@
     total_slots = span_count * span_len
     softmax_scale = (NOPE + ROPE) ** (-0.5)
     query_proj = jnp.dot(
-        lax.all_gather(compressed, "tp", axis=1, tiled=True),
+        jnp.concatenate(
+            lax.all_to_all(jnp.stack([compressed] * lax.axis_size("tp")), "tp", 0, 0), axis=1
+        ),
         w_uq,
         preferred_element_type=jnp.float32,
     )

time: 295 us -> 295 us (level)
  blocking collectives: 25.2 us -> 0 us
  waiting for transfers between devices: 161 us -> 178 us
  starting transfers between devices: 0.08 us -> 6.03 us
    all_gather x1 -> x0, blocking collectives: 25.2 us -> none  [per_device(): lax.all_gather(compressed, 'tp', axis=1, tiled=True)]
    all_gather x1, waiting for transfers between devices: 0.02 us -> 13.5 us  [per_device(): shard_rows = lax.all_gather(w_uk, 'ctx', axis=0, tiled=True)]
    all_to_all x0 -> x1, starting transfers between devices: none -> 5.95 us  [per_device(): lax.all_to_all(jnp.stack([compressed] * lax.axis_size('tp')), 'tp', 0, 0)]
    all_gather x1, waiting for transfers between devices: 72 us -> 75.7 us  [per_device(): shard_rows = lax.all_gather(w_uv, 'ctx', axis=0, tiled=True)]
  transfers between devices with their start and end apart: 3 -> 4, of which waited for: 2 -> 3; matrix products, arithmetic and copies ran while one was open for 22% -> 23% of each run, Pallas kernels for 0% -> 0%
where the time goes in v1:
time: 295 us; the launch traced here: 294 us
  waiting for transfers between devices  178 us (60%)
  other arithmetic  53.4 us (18%)
  matrix products  22.2 us (8%)
  local copies, waits for them, and re-layouts  18.5 us (6%)
  between operations  15.8 us (5%)
  starting transfers between devices  6.03 us (2%)
    all_gather x1, waiting for transfers between devices, per_device(): lax.all_gather(latent, 'ctx', axis=0, tiled=True)  87.4 us
    all_gather x1, waiting for transfers between devices, per_device(): shard_rows = lax.all_gather(w_uv, 'ctx', axis=0, tiled=True)  75.7 us
    add x1, other arithmetic, per_device(): jnp.repeat(span_ids, span_len, total_repeat_length=total_slots) * span_len  36.3 us
    all_gather x1, waiting for transfers between devices, per_device(): shard_rows = lax.all_gather(w_uk, 'ctx', axis=0, tiled=True)  13.5 us
    dot_general x2, matrix products, update(): lax.dot_general(q_matrix, key_rows, (((1,), (1,)), ((), ())), preferred_e...  13.1 us
    gather x4, local copies, waits for them, and re-layouts, per_device(): jnp.repeat(span_ids, span_len, total_repeat_length=total_slots) * span_len  7.81 us
    gather x2, other arithmetic, per_device(): jnp.repeat(span_ids, span_len, total_repeat_length=total_slots) * span_len  7.38 us
    all_to_all x1, starting transfers between devices, per_device(): lax.all_to_all(jnp.stack([compressed] * lax.axis_size('tp')), 'tp', 0, 0)  5.95 us
  transfers between devices with their start and end apart: 4, of which 3 were waited for; matrix products, arithmetic and copies ran while one was open for 23% of the time, Pallas kernels for 0%

profile of v1, /device:TPU:1, one launch (start us, length us, event | category | flops | bytes accessed | tf_op | source)
XLA Modules:
  0.0 294.3 jit_solution(8738837751825066108)
XLA Ops:
  6.5 0.7 all-gather.4.cloned.1.call-update
  7.3 0.7 all-gather.8.cloned.1.call-update
  8.1 1.7 copy.32
  9.8 1.6 stack.2
  11.4 5.9 %all-to-all-start = ((bf16[8,128,192]{1,2,0:T(8,128)(2,1)}), bf16[8,128,192]{1,2,0:T(8,128)(2,1)S(1)}, u32[]{:S(2)}, u32[]{:S(2)}) async-start(bf16[8,128,192]{1,2,0:T(8,128)(2,1)} %stack.2), calls=%async_computation | async-start | bytes 786432 | tf_op jit(solution)/shard_map/all_to_all | solution.py:21
  17.5 0.1 reshape.190
  17.6 1.6 fusion.41
  19.2 2.1 fusion.38
  21.3 2.1 fusion.39
  23.3 2.1 fusion.40
  25.4 0.8 add_add_fusion.3
  26.2 4.5 %compare_select_fusion.1 = (s32[4096,1]{0,1:T(1,128)S(1)}, s32[4096,1]{0,1:T(1,128)S(1)}) fusion(s32[]{:T(128)} %bitcast.63, s32[]{:T(128)} %bitcast.64, s32[]{:T(128)} %bitcast.65, s32[]{:T(128)} %bitcast.66, s32[]{:T(128)} %bitcast.67, s32[]{:T(128)} %bitcast.69, s32[]{:T(128)} %bitcast.68, s32[4096,1]{0,1:T(1,128)S(1)} %bitcast.137, ...), kind=kLoop, calls=%fused_computation.109 | loop fusion | flops 57344 | bytes 65564 | tf_op jit(solution)/shard_map/jit(_take)/gather | solution.py:35
  30.7 2.9 compare_reduce_fusion.56
  33.6 36.3 %multiply_add_fusion = (s32[4096]{0:T(1024)S(1)}, s32[4096]{0:T(1024)S(1)}) fusion(s32[4096]{0:T(1024)S(1)} %tile.14, s32[32,128]{1,0:T(8,128)} %constant.125.clone.1, s32[32]{0:T(128)S(1)} %iota_multiply_fusion, pred[4096]{0:T(1024)(128)(4,1)S(1)} %get-tuple-element.133, pred[4096]{0:T(1024)(128)(4,1)S(1)} %get-tuple-element.132, ...), kind=kLoop, calls=%fused_computation.122 | loop fusion | flops 278528 | bytes 315748 | tf_op jit(solution)/shard_map/add | solution.py:35
  69.9 0.8 add_add_fusion.1
  70.7 0.1 add.86
  70.8 0.1 sub.31
  70.8 0.1 dynamic_slice.3
  70.9 0.7 add_reduce_fusion
  71.6 0.7 slice_reduce_fusion.1
  74.9 3.2 %convolution_convert_fusion = bf16[128,1536]{1,0:T(8,128)(2,1)S(1)} fusion(bf16[128,1536]{0,1:T(8,128)(2,1)S(1)} %bitcast.133, bf16[1536,1536]{1,0:T(8,128)(2,1)} %param.14), kind=kOutput, calls=%fused_computation.38 | convolution fusion | flops 604176384 | bytes 5505024 | tf_op jit(solution)/shard_map/dot_general | solution.py:19
  78.0 0.2 copy.27
  78.3 0.2 copy.41
  78.5 13.5 %all-gather.4.cloned.1.call-done = bf16[512,1024]{1,0:T(8,128)(2,1)} async-done(((bf16[16,1024]{1,0:T(8,128)(2,1)}), bf16[512,1024]{1,0:T(8,128)(2,1)}) %all-gather.4.cloned.1.call-update) | async-done | bytes 1048592 | tf_op jit(solution)/shard_map/all_gather | solution.py:29
  91.9 1.5 copy.29
  93.4 75.7 %all-gather.8.cloned.1.call-done = bf16[512,1024]{1,0:T(8,128)(2,1)} async-done(((bf16[16,1024]{1,0:T(8,128)(2,1)}), bf16[512,1024]{1,0:T(8,128)(2,1)}) %all-gather.8.cloned.1.call-update) | async-done | bytes 1048592 | tf_op jit(solution)/shard_map/all_gather | solution.py:102
  169.2 2.3 copy.37
  171.5 0.5 fusion.30
  172.0 0.1 pad_maximum_fusion
  172.1 87.4 %all-gather.6.cloned.1.call-done = bf16[4096,576]{1,0:T(8,128)(2,1)} async-done(((bf16[128,576]{1,0:T(8,128)(2,1)}), bf16[4096,576]{1,0:T(8,128)(2,1)}) %all-gather.6.cloned.1.call-update) | async-done | bytes 4718608 | tf_op jit(solution)/shard_map/all_gather | solution.py:92
  259.5 13.0 %conditional.2 = (f32[512]{0:T(512)S(1)}, f32[512,512]{1,0:T(8,128)S(1)}) conditional(s32[]{:T(128)} %convert_element_type.36, () %tuple.25, (s32[4096]{0:T(1024)S(1)}, s32[64]{0:T(128)S(1)}, bf16[128,8,576]{2,0,1:T(8,128)(2,1)S(1)}, bf16[4096,576]{1,0:T(8,128)(2,1)}) %tuple.26), branch_computations={%region_2.3_spmd, %region_3.6_spmd} | conditional | flops 4590927360 | bytes 54948160 | solution.py:67
  259.5 0.2 broadcast_compare_fusion
  259.7 0.7 copy.33
  260.5 6.5 %fusion = (f32[512]{0:T(512)S(1)}, f32[512,4096]{1,0:T(8,128)S(1)}) fusion(pred[64,4096]{1,0:T(8,128)(4,1)S(1)} %broadcast_compare_fusion, bf16[4096,576]{1,0:T(8,128)(2,1)} %get-tuple-element.40, bf16[128,8,576]{2,1,0:T(8,128)(2,1)S(1)} %copy.33), kind=kOutput, calls=%fused_computation.2 | convolution fusion | flops 2422210048 | bytes 14026752 | tf_op jit(solution)/shard_map/cond/branch_1_fun/dot_general | solution.py:48
  267.1 2.5 fusion.3
  269.6 2.9 %fusion.2 = f32[512]{0:T(512)S(1)} fusion(f32[512,4096]{1,0:T(8,128)S(1)} %get-tuple-element.141, f32[512]{0:T(512)S(1)} %broadcast_maximum_fusion, pred[64,4096]{1,0:T(8,128)(4,1)S(1)} %broadcast_compare_fusion), kind=kLoop, calls=%fused_computation.4 | loop fusion | flops 10485248 | bytes 8654848 | tf_op jit(solution)/shard_map/cond/branch_1_fun/reduce_sum | solution.py:60
  272.5 0.1 fusion.34
  272.7 0.2 copy.35
  272.9 13.3 %conditional.3 = (f32[512]{0:T(512)S(1)}, f32[512,512]{1,0:T(8,128)S(1)}) conditional(s32[]{:T(128)} %convert_element_type.41, () %tuple.27, (s32[4096]{0:T(1024)S(1)}, s32[64]{0:T(128)S(1)}, bf16[128,8,576]{2,0,1:T(8,128)(2,1)S(1)}, bf16[4096,576]{1,0:T(8,128)(2,1)}) %tuple.28), branch_computations={%region_7.8_spmd, %region_8.11_spmd} | conditional | flops 4590927360 | bytes 54948160 | solution.py:67
  273.1 0.2 broadcast_compare_fusion.1
  273.3 0.7 copy.34
  274.1 6.5 %fusion.15 = (f32[512]{0:T(512)S(1)}, f32[512,4096]{1,0:T(8,128)S(1)}) fusion(pred[64,4096]{1,0:T(8,128)(4,1)S(1)} %broadcast_compare_fusion.1, bf16[4096,576]{1,0:T(8,128)(2,1)} %get-tuple-element.44, bf16[128,8,576]{2,1,0:T(8,128)(2,1)S(1)} %copy.34), kind=kOutput, calls=%fused_computation.21 | convolution fusion | flops 2422210048 | bytes 14026752 | tf_op jit(solution)/shard_map/cond/branch_1_fun/dot_general | solution.py:48
  280.7 2.5 fusion.18
  283.2 2.9 %fusion.17 = f32[512]{0:T(512)S(1)} fusion(f32[512,4096]{1,0:T(8,128)S(1)} %get-tuple-element.143, f32[512]{0:T(512)S(1)} %broadcast_maximum_fusion.1, pred[64,4096]{1,0:T(8,128)(4,1)S(1)} %broadcast_compare_fusion.1), kind=kLoop, calls=%fused_computation.23 | loop fusion | flops 10485248 | bytes 8654848 | tf_op jit(solution)/shard_map/cond/branch_1_fun/reduce_sum | solution.py:60
  286.1 0.1 fusion.35
  286.3 0.2 copy.36
  286.5 0.4 convolution_convert_fusion.2
  286.9 0.9 copy.38
  (24 shorter events, 0.3 us)
Async XLA Ops:
  6.5 85.4 %all-gather.4.cloned.1.call-start = ((), (), s32[]{:S(2)}) async-start(), calls=%async_computation.1 | async-start | bytes 1081344 | tf_op jit(solution)/shard_map/all_gather | solution.py:29
  7.3 161.9 %all-gather.8.cloned.1.call-start = ((), (), s32[]{:S(2)}) async-start(), calls=%async_computation.3 | async-start | bytes 1081344 | tf_op jit(solution)/shard_map/all_gather | solution.py:102
  8.0 251.5 %all-gather.6.cloned.1.call-start = ((), (), s32[]{:S(2)}) async-start(), calls=%async_computation.2 | async-start | bytes 5406720 | tf_op jit(solution)/shard_map/all_gather | solution.py:92
  11.4 63.5 %all-to-all-start = ((bf16[8,128,192]{1,2,0:T(8,128)(2,1)}), bf16[8,128,192]{1,2,0:T(8,128)(2,1)S(1)}, u32[]{:S(2)}, u32[]{:S(2)}) async-start(bf16[8,128,192]{1,2,0:T(8,128)(2,1)} %stack.2), calls=%async_computation | async-start | bytes 786432 | tf_op jit(solution)/shard_map/all_to_all | solution.py:21
  259.7 7.3 %slice-start = ((s8[5242880]{0:T(1024)(128)(4,1)}), s8[4194304]{0:T(1024)(128)(4,1)S(1)}, s32[]{:S(2)}) async-start(s8[5242880]{0:T(1024)(128)(4,1)} %bitcast.139), calls=%async_computation.4 | async-start | bytes 8388608 | tf_op jit(solution)/shard_map/cond
  260.5 6.6 %slice-start.1 = ((s8[5242880]{0:T(1024)(128)(4,1)}), s8[1048576]{0:T(1024)(128)(4,1)S(1)}, s32[]{:S(2)}) async-start(s8[5242880]{0:T(1024)(128)(4,1)} %bitcast.139), calls=%async_computation.5 | async-start | bytes 2097152 | tf_op jit(solution)/shard_map/cond
  272.9 13.6 %copy-start = (bf16[512,1024]{0,1:T(8,128)(2,1)S(1)}, bf16[512,1024]{0,1:T(8,128)(2,1)}, u32[]{:S(2)}) copy-start(bf16[512,1024]{0,1:T(8,128)(2,1)} %copy.37) | copy-start | bytes 3145732
  273.3 7.3 %slice-start.2 = ((s8[5242880]{0:T(1024)(128)(4,1)}), s8[4194304]{0:T(1024)(128)(4,1)S(1)}, s32[]{:S(2)}) async-start(s8[5242880]{0:T(1024)(128)(4,1)} %bitcast.141), calls=%async_computation.6 | async-start | bytes 8388608 | tf_op jit(solution)/shard_map/cond
  274.1 6.6 %slice-start.3 = ((s8[5242880]{0:T(1024)(128)(4,1)}), s8[1048576]{0:T(1024)(128)(4,1)S(1)}, s32[]{:S(2)}) async-start(s8[5242880]{0:T(1024)(128)(4,1)} %bitcast.141), calls=%async_computation.7 | async-start | bytes 2097152 | tf_op jit(solution)/shard_map/cond
Sparse Core Ops, SparseCore 0:
  10.1 81.7 all-gather.3
  94.7 74.4 all-gather.7
  171.9 87.5 all-gather.5
